TPU v7x, 32 devices: a whole 2x2x4 slice. The times are simulated.
32 devices in a mesh: batch: 4 (over x, core), vocab: 8 (over z, y).
Axes of the slice: x: 2, y: 2, z: 4, core: 2. Of those that a mesh axis runs over, the one named last changes fastest.
Arguments:
- logits: float32 [256, 152064], P('batch', 'vocab'), may hold values from -18 to 350
- history: int32 [256, 4096], P('batch', 'vocab'), may hold values from 0 to 152063, as said below
- history_weight: bfloat16 [256, 4096], P('batch', 'vocab'), may hold values from 0.25 to 2
- lengths: int32 [256], P('batch'), may hold values from 1 to 4096
- repetition: float32 [256], P('batch'), may hold values from 1.1 to 2
- frequency: float32 [256], P('batch'), may hold values from 0.05 to 0.5
- presence: float32 [256], P('batch'), may hold values from 0.1 to 1.5
Outputs:
- log_probs: float32 [256, 152064], P('batch', 'vocab')
Inputs may be any that keep to these rules, and one draw needn't show every extreme that they name: `history`: split each sequence's positions into 8 aligned blocks of equal length and the vocabulary into 8 equal ranges: within one block at most 128 ids fall in any one range.
All inputs are finite; a program needn't handle non-finite values.
Results may differ from a plain program's by a relative error of at most 0.0003.
Values may be sent and summed in bfloat16 or wider, within the bound.
No kernel may reach another device: no remote copies, remote signals or barrier semaphores. Data moves between devices by JAX's collectives and lax.ppermute only.
A program may use at most 64 MiB of HBM per device.

v0:
```python
import functools

import jax
import jax.numpy as jnp
from jax import lax
from jax.experimental import pallas as pl
from jax.experimental.pallas import tpu as pltpu
from jax.sharding import PartitionSpec as P

LANES = 128
FIRST = 4
SECOND = 5
TOGETHER = 4
CHUNK = 128
HALVES = CHUNK // LANES
LOG2E = 1.4426950408889634
LN2 = 0.6931471805599453
LEAST = 1e-20
FIELD = 16
SCALE = 512.0


def pick(table, place):
    return lax.gather(
        table,
        place[:, :, None],
        lax.GatherDimensionNumbers(
            offset_dims=(),
            collapsed_slice_dims=(1,),
            start_index_map=(1,),
            operand_batching_dims=(0,),
            start_indices_batching_dims=(0,),
        ),
        slice_sizes=(1, 1),
        mode=lax.GatherScatterMode.PROMISE_IN_BOUNDS,
    )


def column(row, rows):
    wide = jnp.broadcast_to(row, (rows, rows))
    same = lax.broadcasted_iota(jnp.int32, (rows, rows), 0) == lax.broadcasted_iota(
        jnp.int32, (rows, rows), 1
    )
    return jnp.sum(jnp.where(same, wide, 0.0), axis=1, keepdims=True)


def pack_kernel(
    shards, slots, width, ids_hbm, weight_hbm, lengths_hbm, send_ref, ids_ref, weight_ref, lengths_ref, sem
):
    copies = [
        pltpu.make_async_copy(source, target, sem.at[k])
        for k, (source, target) in enumerate(
            ((ids_hbm, ids_ref), (weight_hbm, weight_ref), (lengths_hbm, lengths_ref))
        )
    ]
    for copy in copies:
        copy.start()
    for copy in copies:
        copy.wait()
    rows, span = ids_ref.shape
    tiles = span // LANES
    first = lax.axis_index("vocab") * span
    ids = ids_ref[...]
    lengths = column(lengths_ref[...].astype(jnp.float32), rows)
    positions = (lax.broadcasted_iota(jnp.int32, (rows, span), 1) + first).astype(jnp.float32)
    valid = positions < lengths
    owner = jnp.zeros_like(ids)
    for shard in range(1, shards):
        owner = owner + (ids >= shard * width).astype(jnp.int32)
    code = (weight_ref[...].astype(jnp.float32) * SCALE).astype(jnp.int32)
    payload = ((ids - owner * width) << FIELD) | code
    owner = jnp.where(valid, owner, -1)
    payloads = [payload[:, t * LANES : (t + 1) * LANES] for t in range(tiles)]
    below = lax.broadcasted_iota(jnp.int32, (LANES, LANES), 0) <= lax.broadcasted_iota(
        jnp.int32, (LANES, LANES), 1
    )
    below = jnp.where(below, 1.0, 0.0)
    low = min(tiles, 3)
    below = [(below * float(256**t)).astype(jnp.bfloat16) for t in range(low)]
    stacked = jnp.concatenate(below, axis=0)
    lane = lax.broadcasted_iota(jnp.int32, (rows, LANES), 1)
    last = jnp.full((rows, LANES), LANES - 1, jnp.int32)

    def place(shard):
        mine = jnp.where(owner == shard, 1.0, 0.0).astype(jnp.bfloat16)
        word = jnp.dot(
            mine[:, : low * LANES], stacked, preferred_element_type=jnp.float32
        ).astype(jnp.int32)
        for t in range(low, tiles):
            high = jnp.dot(
                mine[:, t * LANES : (t + 1) * LANES], below[0], preferred_element_type=jnp.float32
            )
            word = word | (high.astype(jnp.int32) << (8 * t))
        totals = pick(word, last)
        start = totals & 255
        base = jnp.zeros_like(lane)
        lift = jnp.full_like(lane, 24)
        later = []
        for t in range(1, tiles):
            past = lane >= start
            later.append(past)
            base = jnp.where(past, start, base)
            lift = jnp.where(past, 24 - 8 * t, lift)
            start = start + ((totals >> (8 * t)) & 255)
        limit = ((lane - base) << 24) | 0xFFFFFF
        spot = jnp.full_like(lane, -1)
        step = LANES // 2
        while step:
            probe = spot + step
            spot = jnp.where((pick(word, probe) << lift) <= limit, probe, spot)
            step //= 2
        spot = spot + 1
        found = pick(payloads[0], spot)
        for past, other in zip(later, payloads[1:]):
            found = jnp.where(past, pick(other, spot), found)
        send_ref[shard] = jnp.where(lane < start, found, 0)[:, :slots]

    def some(step, carry):
        for k in range(TOGETHER):
            place(step * TOGETHER + k)
        return carry

    lax.fori_loop(0, shards // TOGETHER, some, 0)


def prepare_kernel(
    logits_hbm, repetition_hbm, frequency_hbm, presence_hbm, plain_hbm, seen_hbm, shift_ref, rate_ref,
    logits, plain_ref, seen_ref, factors, logits_sem, factor_sem, plain_sem, seen_sem,
):
    rows, width = plain_ref.shape
    groups = rows // 8
    tiles = -(-width // LANES)
    loads = [
        pltpu.make_async_copy(
            logits_hbm.at[pl.ds(group * 8, 8)], logits.at[pl.ds(group * 8, 8)], logits_sem.at[group]
        )
        for group in range(groups)
    ]
    fetches = [
        pltpu.make_async_copy(ref, factors.at[pl.ds(k, 1)], factor_sem.at[k])
        for k, ref in enumerate((repetition_hbm, frequency_hbm, presence_hbm))
    ]
    for copy in fetches + loads:
        copy.start()
    for fetch in fetches:
        fetch.wait()
    repetition = column(factors[0:1, :], rows)
    rate_ref[...] = jnp.broadcast_to(column(factors[1:2, :], rows) * LOG2E, rate_ref.shape)
    presence = column(factors[2:3, :], rows) * LOG2E
    above, below = LOG2E / repetition, LOG2E * repetition
    stores = []
    for group in range(groups):
        loads[group].wait()
        part = slice(group * 8, group * 8 + 8)
        best = jnp.full((8, LANES), -jnp.inf, jnp.float32)
        tail = None
        for tile in range(tiles):
            size = min(LANES, width - tile * LANES)
            x = logits[part, tile * LANES : tile * LANES + size]
            if size == LANES:
                best = jnp.maximum(best, x)
            else:
                tail = jnp.max(x, axis=1, keepdims=True)
        top = jnp.max(best, axis=1, keepdims=True)
        if tail is not None:
            top = jnp.maximum(top, tail)
        shift = top * LOG2E
        shift_ref[part, :] = jnp.broadcast_to(shift, (8, shift_ref.shape[1]))
        offset = shift + presence[part]
        over, under = above[part], below[part]
        for tile in range(tiles):
            size = min(LANES, width - tile * LANES)
            columns = slice(tile * LANES, tile * LANES + size)
            x = logits[part, columns]
            plain_ref[part, columns] = x * LOG2E - shift
            seen_ref[part, columns] = x * jnp.where(x > 0, over, under) - offset
        stores.append(pltpu.make_async_copy(plain_ref.at[part], plain_hbm.at[part], plain_sem.at[group]))
        stores.append(pltpu.make_async_copy(seen_ref.at[part], seen_hbm.at[part], seen_sem.at[group]))
        for store in stores[-2:]:
            store.start()
    for store in stores:
        store.wait()


def tally_kernel(
    ordered, got_ref, plain_hbm, seen_hbm, shift_ref, rate_ref, adjusted_ref, stats_ref,
    seen_ref, dense_a, dense_b, sums_a, sums_b, trips, plain_sem, seen_sem,
):
    blocks, rows, _ = got_ref.shape
    width = plain_hbm.shape[1]
    groups = rows // 8
    tiles = -(-width // LANES)
    uppers = -(-(-(-width // CHUNK)) // 16) * 16
    first, second = min(FIRST, blocks), min(SECOND, blocks)
    dense, sums = (dense_a, dense_b), (sums_a, sums_b)

    def rows_of(group):
        return pl.ds(pl.multiple_of(group * 8, 8), 8)

    def loads(group):
        part = rows_of(group)
        return (
            pltpu.make_async_copy(plain_hbm.at[part], adjusted_ref.at[part], plain_sem.at[group]),
            pltpu.make_async_copy(seen_hbm.at[part], seen_ref.at[part], seen_sem.at[group]),
        )

    for group in range(groups):
        for copy in loads(group):
            copy.start()

    lane = lax.broadcasted_iota(jnp.int32, (8, LANES), 1)
    ones = jnp.ones((LANES, LANES), jnp.bfloat16)

    def keep(side, tile, word):
        local = word >> FIELD
        fields = (local // CHUNK, local & (CHUNK - 1), word & 0xFFFF)
        for k, field in enumerate(fields):
            value = field.astype(jnp.float32)
            dense[side][k, pl.ds(tile * 8, 8), :] = value * (1.0 / SCALE) if k == 2 else value

    def merge(group, side):
        words = [got_ref[block, rows_of(group), :] for block in range(blocks)]
        if not ordered:
            for block in range(blocks):
                keep(side, block, words[block])
            trips[side] = blocks
            return
        full = jnp.concatenate(words, axis=0) > 0
        count = jnp.dot(
            jnp.where(full, 1.0, 0.0).astype(jnp.bfloat16), ones, preferred_element_type=jnp.float32
        ).astype(jnp.int32)
        starts = [jnp.zeros_like(lane)]
        for block in range(blocks):
            starts.append(starts[-1] + count[block * 8 : block * 8 + 8])
        turned = [
            pick(words[block], (lane - starts[block]) & (LANES - 1))
            for block in range(blocks)
        ]
        for tile in range(blocks):
            spot = lane + tile * LANES
            value = turned[tile]
            for block in range(tile + 1, blocks):
                value = jnp.where(spot >= starts[block], turned[block], value)
            keep(side, tile, jnp.where(spot < starts[blocks], value, 0))
        trips[side] = (jnp.max(starts[blocks]) + LANES - 1) // LANES

    iota = lax.broadcasted_iota(jnp.int32, (max(CHUNK, uppers), LANES), 0).astype(jnp.float32)
    iota = iota.astype(jnp.bfloat16)
    zero = jnp.zeros((), jnp.bfloat16)
    one = jnp.ones((), jnp.bfloat16)

    def product(side, row, first_tile, count):
        def spread(k, tile, size):
            piece = dense[side][k, pl.ds(tile * 8 + row, 8, stride=0), :]
            piece = jnp.concatenate([piece, piece], axis=0).astype(jnp.bfloat16)
            return jnp.concatenate([piece] * (size // 16), axis=0)

        hot_upper, hot_lower = [], []
        for step in range(count):
            tile = first_tile + step
            hot_upper.append(jnp.where(spread(0, tile, uppers) == iota[:uppers], one, zero))
            hot_lower.append(jnp.where(spread(1, tile, CHUNK) == iota[:CHUNK], spread(2, tile, CHUNK), zero))
        return lax.dot_general(
            jnp.concatenate(hot_upper, axis=1),
            jnp.concatenate(hot_lower, axis=1),
            (((1,), (1,)), ((), ())),
            preferred_element_type=jnp.float32,
        )

    def tally_row(side, row, count):
        total = product(side, row, 0, count)
        for half in range(HALVES):
            part = total[:, half * LANES : (half + 1) * LANES]
            sums[side][half, pl.ds(row, uppers, stride=8), :] = part

    def tally_rest(side):
        def more(tile, carry):
            for row in range(8):
                total = product(side, row, tile, 1)
                for half in range(HALVES):
                    part = total[:, half * LANES : (half + 1) * LANES]
                    sums[side][half, pl.ds(row, uppers, stride=8), :] += part
            return carry

        if blocks > second:
            lax.fori_loop(second, trips[side], more, 0)

    line = lax.broadcasted_iota(jnp.int32, (8, 2 * rows), 1)
    inner = lax.broadcasted_iota(jnp.int32, (8, 2 * rows), 0)

    def place(spot, group, shift, rest):
        seq = group * 8 + inner
        return spot + jnp.where(line == seq, shift, 0.0) + jnp.where(line == seq + rows, rest, 0.0)

    def both(group, side, spot, following=None):
        for copy in loads(group):
            copy.wait()
        return either(1 - side, lambda count: part_of(group, side, spot, count, following))

    def either(side, run):
        if second == first:
            return run(first)
        return lax.cond(trips[side] > first, lambda: run(second), lambda: run(first))

    def part_of(group, side, spot, count, following):
        if following is not None:
            merge(following, side)
        part = rows_of(group)
        rate = rate_ref[part, :]
        total = jnp.zeros((8, LANES), jnp.float32)
        rest = jnp.zeros((8, 1), jnp.float32)
        share = -(-tiles // 8)
        for row in range(8):
            for tile in range(row * share, min(tiles, (row + 1) * share)):
                size = min(LANES, width - tile * LANES)
                columns = pl.ds(tile * LANES, size)
                chunk, half = divmod(tile, HALVES)
                weighted = sums[side][half, chunk * 8 : chunk * 8 + 8, :size]
                value = jnp.where(
                    weighted > 0, seen_ref[part, columns] - rate[:, :size] * weighted, adjusted_ref[part, columns]
                )
                adjusted_ref[part, columns] = value
                value = jnp.exp2(value)
                if size == LANES:
                    total = total + value
                else:
                    rest = jnp.sum(value, axis=1, keepdims=True)
            if count:
                tally_row(1 - side, row, count)
        rest = rest + jnp.sum(total, axis=1, keepdims=True)
        return place(spot, group, shift_ref[part, :], rest)

    def renew(group, spot):
        part = rows_of(group)
        value = adjusted_ref[part, :]
        top = jnp.max(value, axis=1, keepdims=True)
        rest = jnp.sum(jnp.exp2(value - top), axis=1, keepdims=True)
        return place(spot, group, shift_ref[part, :] + top, rest)

    def begin(count):
        merge(1, 1)
        for row in range(8):
            tally_row(0, row, count)

    merge(0, 0)
    either(0, begin)
    tally_rest(0)

    def two(pair, spot):
        for side in range(2):
            group = pair * 2 + side
            spot = both(group, side, spot, group + 2)
            tally_rest(1 - side)
        return spot

    empty = jnp.zeros((8, 2 * rows), jnp.float32)
    spot = lax.fori_loop(0, groups // 2 - 1, two, empty)
    spot = both(groups - 2, 0, spot)
    tally_rest(1)
    for copy in loads(groups - 1):
        copy.wait()
    spot = part_of(groups - 1, 1, spot, 0, None)
    spot = jnp.sum(spot, axis=0, keepdims=True)
    stats_ref[...] = jnp.broadcast_to(spot, stats_ref.shape)

    @pl.when(jnp.min(jnp.where(line[:1] < rows, 1.0, spot)) < LEAST)
    def _():
        exact = jnp.sum(lax.fori_loop(0, groups, renew, empty), axis=0, keepdims=True)
        stats_ref[...] = jnp.broadcast_to(exact, stats_ref.shape)


def finish_kernel(adjusted_ref, shift_ref, stats_ref, out_ref, result, sem):
    rows = adjusted_ref.shape[0]
    tops = stats_ref[:, :rows]
    totals = stats_ref[:, rows:]
    top = jnp.max(tops, axis=0, keepdims=True)
    total = jnp.sum(totals * jnp.exp2(tops - top), axis=0, keepdims=True)
    offset = shift_ref[:, :1] - column(top, rows)
    offset = offset * LN2 - column(jnp.log(total), rows)
    copies = []
    for group in range(rows // 8):
        part = slice(group * 8, group * 8 + 8)
        result[part, :] = adjusted_ref[part, :] * LN2 + offset[part]
        copies.append(pltpu.make_async_copy(result.at[part], out_ref.at[part], sem.at[group]))
        copies[-1].start()
    for copy in copies:
        copy.wait()


def vmem(shape, dtype):
    return pltpu.VMEM(shape, dtype)


def outside(array):
    return pltpu.with_memory_space_constraint(array, pltpu.HBM)


def body(logits, history, history_weight, lengths, repetition, frequency, presence):
    rows, width = logits.shape
    span = history.shape[1]
    shards = lax.axis_size("vocab")
    slots = max(2, 2 * span // shards)
    full = pl.BlockSpec(memory_space=pltpu.VMEM)
    away = pl.BlockSpec(memory_space=pltpu.HBM)
    ordered = slots % LANES == 0
    send = pl.pallas_call(
        functools.partial(pack_kernel, shards, slots, width),
        out_shape=vmem((shards, rows, slots), jnp.int32),
        in_specs=[away] * 3,
        out_specs=full,
        scratch_shapes=[
            vmem((rows, span), jnp.int32),
            vmem((rows, span), jnp.bfloat16),
            vmem((1, rows), jnp.int32),
            pltpu.SemaphoreType.DMA((3,)),
        ],
        compiler_params=pltpu.CompilerParams(vmem_limit_bytes=8 << 20),
        name="pack",
    )(outside(history), outside(history_weight), outside(lengths.reshape(1, rows)))
    got = lax.all_to_all(send, "vocab", split_axis=0, concat_axis=0, tiled=True)
    if ordered:
        got = got.reshape(shards, rows, slots // LANES, LANES).transpose(0, 2, 1, 3)
        got = got.reshape(-1, rows, LANES)
    else:
        got = got.transpose(1, 0, 2).reshape(rows, shards * slots)
        got = jnp.pad(got, ((0, 0), (0, -(shards * slots) % LANES)))
        got = got.reshape(rows, -1, LANES).transpose(1, 0, 2)
    got = jnp.pad(got, ((0, got.shape[0] % 2), (0, 0), (0, 0)))
    groups = rows // 8
    uppers = -(-(-(-width // CHUNK)) // 16) * 16
    wide = vmem((rows, width), jnp.float32)
    plain, seen, shift, rate = pl.pallas_call(
        prepare_kernel,
        out_shape=(
            pltpu.HBM((rows, width), jnp.float32),
            pltpu.HBM((rows, width), jnp.float32),
            vmem((rows, 2 * rows), jnp.float32),
            vmem((rows, LANES), jnp.float32),
        ),
        in_specs=[away] * 4,
        out_specs=(away, away, full, full),
        scratch_shapes=[
            wide,
            wide,
            wide,
            vmem((3, rows), jnp.float32),
            pltpu.SemaphoreType.DMA((groups,)),
            pltpu.SemaphoreType.DMA((3,)),
            pltpu.SemaphoreType.DMA((groups,)),
            pltpu.SemaphoreType.DMA((groups,)),
        ],
        compiler_params=pltpu.CompilerParams(vmem_limit_bytes=24 << 20),
        cost_estimate=pl.CostEstimate(
            flops=400 * rows * width, bytes_accessed=400 * rows * width, transcendentals=0
        ),
        name="prepare",
    )(
        outside(logits),
        outside(repetition.reshape(1, rows)),
        outside(frequency.reshape(1, rows)),
        outside(presence.reshape(1, rows)),
    )
    adjusted, stats = pl.pallas_call(
        functools.partial(tally_kernel, ordered),
        out_shape=(wide, vmem((shards, 2 * rows), jnp.float32)),
        in_specs=[full, away, away, full, full],
        out_specs=(full, full),
        scratch_shapes=[
            wide,
            *[vmem((3, got.shape[0] * 8, LANES), jnp.float32)] * 2,
            *[vmem((HALVES, uppers * 8, LANES), jnp.float32)] * 2,
            pltpu.SMEM((2,), jnp.int32),
            pltpu.SemaphoreType.DMA((groups,)),
            pltpu.SemaphoreType.DMA((groups,)),
        ],
        compiler_params=pltpu.CompilerParams(vmem_limit_bytes=16 << 20),
        name="tally",
    )(got, outside(plain), outside(seen), shift, rate)
    stats = lax.all_to_all(stats, "vocab", split_axis=0, concat_axis=0, tiled=True)
    return pl.pallas_call(
        finish_kernel,
        out_shape=jax.ShapeDtypeStruct((rows, width), jnp.float32),
        in_specs=[full] * 3,
        out_specs=away,
        scratch_shapes=[wide, pltpu.SemaphoreType.DMA((groups,))],
        compiler_params=pltpu.CompilerParams(vmem_limit_bytes=16 << 20),
        name="finish",
    )(adjusted, shift, stats)


def solution(mesh):
    return jax.shard_map(
        body,
        mesh=mesh,
        in_specs=(
            P("batch", "vocab"),
            P("batch", "vocab"),
            P("batch", "vocab"),
            P("batch"),
            P("batch"),
            P("batch"),
            P("batch"),
        ),
        out_specs=P("batch", "vocab"),
        check_vma=False,
    )
```

profile of v0, /device:TPU:0, one launch (start us, length us, event | category | flops | bytes accessed | tf_op | source)
XLA Modules:
  0.0 39.4 jit_solution(5159647710617923739)
XLA Ops:
  0.0 4.1 %pack.1 = s32[8,64,128]{2,1,0:T(8,128)} custom-call(s32[64,512]{1,0:T(8,128)} %ids_hbm.1, bf16[64,512]{1,0:T(8,128)(2,1)} %weight_hbm.1, s32[1,64]{1,0:T(1,128)} %bitcast.13), custom_call_target="tpu_custom_call" | custom-call | tf_op jit(solution)/shard_map/pack/pallas_call | solution.py:406
  4.1 7.3 %all-to-all-start = ((s32[8,64,128]{2,1,0:T(8,128)}), s32[8,64,128]{2,1,0:T(8,128)S(1)}, u32[]{:S(2)}, u32[]{:S(2)}) async-start(s32[8,64,128]{2,1,0:T(8,128)} %pack.1), calls=%async_computation | async-start | bytes 524288 | tf_op jit(solution)/shard_map/all_to_all | solution.py:420
  11.4 6.3 %prepare.1 = (f32[64,19008]{1,0:T(8,128)}, f32[64,19008]{1,0:T(8,128)}, f32[64,128]{1,0:T(8,128)S(1)}, f32[64,128]{1,0:T(8,128)S(1)}) custom-call(f32[64,19008]{1,0:T(8,128)} %logits_hbm.1, f32[1,64]{1,0:T(1,128)} %bitcast.10, f32[1,64]{1,0:T(1,128)} %bitcast.11, f32[1,64]{1,0:T(1,128)} %bitcast.12), custom_call_target="tpu_custom_call" | custom-call | flops 486604800 | bytes 486604800 | tf_op jit(solution)/shard_map/prepare/pallas_call | solution.py:432
  17.8 2.6 %all-to-all-done.got_ref = s32[8,64,128]{2,1,0:T(8,128)S(1)} async-done(((s32[8,64,128]{2,1,0:T(8,128)}), s32[8,64,128]{2,1,0:T(8,128)S(1)}, u32[]{:S(2)}, u32[]{:S(2)}) %all-to-all-start) | async-done | bytes 262176 | tf_op jit(solution)/shard_map/all_to_all | solution.py:420
  20.4 6.5 %tally.1 = (f32[64,19008]{1,0:T(8,128)S(1)}, f32[8,128]{1,0:T(8,128)S(1)}) custom-call(s32[8,64,128]{2,1,0:T(8,128)S(1)} %all-to-all-done.got_ref, f32[64,19008]{1,0:T(8,128)} %get-tuple-element.11.plain_hbm, f32[64,19008]{1,0:T(8,128)} %get-tuple-element.12.seen_hbm, f32[64,128]{1,0:T(8,128)S(1)} %get-tuple-element.13.shift_ref, ...), custom_call_target="tpu_custom_call" | custom-call | tf_op jit(solution)/shard_map/tally/pallas_call | solution.py:463
  26.9 9.9 %all_to_all.16 = f32[8,1,128]{2,1,0:T(1,128)S(1)} all-to-all(f32[8,1,128]{2,1,0:T(1,128)S(1)} %bitcast.9), channel_id=1, replica_groups=mesh['batch'=4,'vocab'=8] {'vocab'}, dimensions={0} | all-to-all | bytes 8192 | tf_op jit(solution)/shard_map/all_to_all | solution.py:479
  36.8 2.7 %finish.1 = f32[64,19008]{1,0:T(8,128)} custom-call(f32[64,19008]{1,0:T(8,128)S(1)} %get-tuple-element.15.adjusted_ref, f32[64,128]{1,0:T(8,128)S(1)} %get-tuple-element.13.shift_ref, f32[8,128]{1,0:T(8,128)S(1)} %bitcast.8), custom_call_target="tpu_custom_call" | custom-call | tf_op jit(solution)/shard_map/finish/pallas_call | solution.py:480
Async XLA Ops:
  4.1 16.2 %all-to-all-start = ((s32[8,64,128]{2,1,0:T(8,128)}), s32[8,64,128]{2,1,0:T(8,128)S(1)}, u32[]{:S(2)}, u32[]{:S(2)}) async-start(s32[8,64,128]{2,1,0:T(8,128)} %pack.1), calls=%async_computation | async-start | bytes 524288 | tf_op jit(solution)/shard_map/all_to_all | solution.py:420
where the time goes:
time: 39.7 us; the launch traced here: 39.4 us
  Pallas kernels  19.6 us (49%)
  blocking collectives  9.86 us (25%)
  starting transfers between devices  7.32 us (18%)
  waiting for transfers between devices  2.6 us (7%)
    all_to_all x1, blocking collectives, body(): lax.all_to_all(stats, 'vocab', split_axis=0, concat_axis=0, tiled=True)  9.86 us
    all_to_all x1, starting transfers between devices, body(): got = lax.all_to_all(send, 'vocab', split_axis=0, concat_axis=0, tiled=True)  7.32 us
    pallas_call x1, Pallas kernels, body(): pl.pallas_call(functools.partial(tally_kernel, ordered), out_shape=(wide,...  6.54 us
    pallas_call x1, Pallas kernels, body(): pl.pallas_call(prepare_kernel, out_shape=(pltpu.HBM((rows, width), jnp.fl...  6.31 us
    pallas_call x1, Pallas kernels, body(): pl.pallas_call(functools.partial(pack_kernel, shards, slots, width), out_...  4.11 us
    pallas_call x1, Pallas kernels, body(): pl.pallas_call(finish_kernel, out_shape=jax.ShapeDtypeStruct((rows, width...  2.68 us
    all_to_all x1, waiting for transfers between devices, body(): got = lax.all_to_all(send, 'vocab', split_axis=0, concat_axis=0, tiled=True)  2.6 us
  transfers between devices with their start and end apart: 1, of which 1 were waited for; matrix products, arithmetic and copies ran while one was open for 0% of the time, Pallas kernels for 16%

commit v1 on v0

--- a/solution.py
+++ b/solution.py
@@ -8,8 +8,7 @@
 from jax.sharding import PartitionSpec as P
 
 LANES = 128
-FIRST = 4
-SECOND = 5
+PROFILE = (2, 2, 3, 3, 4, 4, 4, 5)
 TOGETHER = 4
 CHUNK = 128
 HALVES = CHUNK // LANES
@@ -184,14 +183,15 @@
 
 def tally_kernel(
     ordered, got_ref, plain_hbm, seen_hbm, shift_ref, rate_ref, adjusted_ref, stats_ref,
-    seen_ref, dense_a, dense_b, sums_a, sums_b, trips, plain_sem, seen_sem,
+    seen_ref, dense_a, dense_b, sums_a, sums_b, trips, order, misfit, plain_sem, seen_sem,
 ):
     blocks, rows, _ = got_ref.shape
     width = plain_hbm.shape[1]
     groups = rows // 8
     tiles = -(-width // LANES)
     uppers = -(-(-(-width // CHUNK)) // 16) * 16
-    first, second = min(FIRST, blocks), min(SECOND, blocks)
+    caps = [min(cap, blocks) for cap in PROFILE]
+    second = max(caps)
     dense, sums = (dense_a, dense_b), (sums_a, sums_b)
 
     def rows_of(group):
@@ -209,6 +209,7 @@
             copy.start()
 
     lane = lax.broadcasted_iota(jnp.int32, (8, LANES), 1)
+    sub = lax.broadcasted_iota(jnp.int32, (8, LANES), 0)
     ones = jnp.ones((LANES, LANES), jnp.bfloat16)
 
     def keep(side, tile, word):
@@ -242,7 +243,19 @@
             for block in range(tile + 1, blocks):
                 value = jnp.where(spot >= starts[block], turned[block], value)
             keep(side, tile, jnp.where(spot < starts[blocks], value, 0))
-        trips[side] = (jnp.max(starts[blocks]) + LANES - 1) // LANES
+        have = starts[blocks]
+        trips[side] = (jnp.max(have) + LANES - 1) // LANES
+        across = jnp.sum(jnp.where(lane == sub, have.astype(jnp.float32), 0.0), axis=0, keepdims=True)
+        across = jnp.broadcast_to(across, (8, LANES)).astype(jnp.int32)
+        fewer = ((across < have) | ((across == have) & (lane < sub))) & (lane < 8)
+        rank = jnp.sum(jnp.where(fewer, 1.0, 0.0), axis=1, keepdims=True)
+        rank = jnp.broadcast_to(rank, (8, LANES)).astype(jnp.int32)
+        cap = jnp.full_like(lane, caps[0])
+        for slot in range(8):
+            order[side * 8 + slot] = jnp.max(jnp.where(rank == slot, sub, 0))
+            if slot and caps[slot] != caps[slot - 1]:
+                cap = jnp.where(rank >= slot, caps[slot], cap)
+        misfit[side] = jnp.max(jnp.where(have > cap * LANES, 1, 0))
 
     iota = lax.broadcasted_iota(jnp.int32, (max(CHUNK, uppers), LANES), 0).astype(jnp.float32)
     iota = iota.astype(jnp.bfloat16)
@@ -295,19 +308,24 @@
     def both(group, side, spot, following=None):
         for copy in loads(group):
             copy.wait()
-        return either(1 - side, lambda count: part_of(group, side, spot, count, following))
+        return either(1 - side, lambda counts: part_of(group, side, spot, counts, following))
 
     def either(side, run):
-        if second == first:
-            return run(first)
-        return lax.cond(trips[side] > first, lambda: run(second), lambda: run(first))
-
-    def part_of(group, side, spot, count, following):
+        plainly = [(row, second) for row in range(8)]
+        if not ordered:
+            return run(plainly)
+        return lax.cond(
+            misfit[side] > 0,
+            lambda: run(plainly),
+            lambda: run([(order[side * 8 + slot], caps[slot]) for slot in range(8)]),
+        )
+
+    def part_of(group, side, spot, counts, following):
         if following is not None:
             merge(following, side)
         part = rows_of(group)
         rate = rate_ref[part, :]
-        total = jnp.zeros((8, LANES), jnp.float32)
+        totals = [jnp.zeros((8, LANES), jnp.float32)] * 4
         rest = jnp.zeros((8, 1), jnp.float32)
         share = -(-tiles // 8)
         for row in range(8):
@@ -322,11 +340,12 @@
                 adjusted_ref[part, columns] = value
                 value = jnp.exp2(value)
                 if size == LANES:
-                    total = total + value
+                    totals[tile % 4] = totals[tile % 4] + value
                 else:
                     rest = jnp.sum(value, axis=1, keepdims=True)
-            if count:
-                tally_row(1 - side, row, count)
+            if counts:
+                tally_row(1 - side, *counts[row])
+        total = (totals[0] + totals[1]) + (totals[2] + totals[3])
         rest = rest + jnp.sum(total, axis=1, keepdims=True)
         return place(spot, group, shift_ref[part, :], rest)
 
@@ -337,9 +356,9 @@
         rest = jnp.sum(jnp.exp2(value - top), axis=1, keepdims=True)
         return place(spot, group, shift_ref[part, :] + top, rest)
 
-    def begin(count):
+    def begin(counts):
         merge(1, 1)
-        for row in range(8):
+        for row, count in counts:
             tally_row(0, row, count)
 
     merge(0, 0)
@@ -359,7 +378,7 @@
     tally_rest(1)
     for copy in loads(groups - 1):
         copy.wait()
-    spot = part_of(groups - 1, 1, spot, 0, None)
+    spot = part_of(groups - 1, 1, spot, [], None)
     spot = jnp.sum(spot, axis=0, keepdims=True)
     stats_ref[...] = jnp.broadcast_to(spot, stats_ref.shape)
 
@@ -470,6 +489,8 @@
             *[vmem((3, got.shape[0] * 8, LANES), jnp.float32)] * 2,
             *[vmem((HALVES, uppers * 8, LANES), jnp.float32)] * 2,
             pltpu.SMEM((2,), jnp.int32),
+            pltpu.SMEM((16,), jnp.int32),
+            pltpu.SMEM((2,), jnp.int32),
             pltpu.SemaphoreType.DMA((groups,)),
             pltpu.SemaphoreType.DMA((groups,)),
         ],

time: 39.7 us -> 39.9 us (level)
  no operation moved by 1% of the time
where the time goes in v1:
time: 39.9 us; the launch traced here: 39.4 us
  Pallas kernels  19.6 us (49%)
  blocking collectives  9.87 us (25%)
  starting transfers between devices  7.32 us (18%)
  waiting for transfers between devices  2.6 us (7%)
    all_to_all x1, blocking collectives, body(): lax.all_to_all(stats, 'vocab', split_axis=0, concat_axis=0, tiled=True)  9.87 us
    all_to_all x1, starting transfers between devices, body(): got = lax.all_to_all(send, 'vocab', split_axis=0, concat_axis=0, tiled=True)  7.32 us
    pallas_call x1, Pallas kernels, body(): pl.pallas_call(functools.partial(tally_kernel, ordered), out_shape=(wide,...  6.47 us
    pallas_call x1, Pallas kernels, body(): pl.pallas_call(prepare_kernel, out_shape=(pltpu.HBM((rows, width), jnp.fl...  6.31 us
    pallas_call x1, Pallas kernels, body(): pl.pallas_call(functools.partial(pack_kernel, shards, slots, width), out_...  4.11 us
    pallas_call x1, Pallas kernels, body(): pl.pallas_call(finish_kernel, out_shape=jax.ShapeDtypeStruct((rows, width...  2.68 us
    all_to_all x1, waiting for transfers between devices, body(): got = lax.all_to_all(send, 'vocab', split_axis=0, concat_axis=0, tiled=True)  2.6 us
  transfers between devices with their start and end apart: 1, of which 1 were waited for; matrix products, arithmetic and copies ran while one was open for 0% of the time, Pallas kernels for 16%

profile of v1, /device:TPU:0, one launch (start us, length us, event | category | flops | bytes accessed | tf_op | source)
XLA Modules:
  0.0 39.4 jit_solution(17820657494002172652)
XLA Ops:
  0.0 4.1 %pack.1 = s32[8,64,128]{2,1,0:T(8,128)} custom-call(s32[64,512]{1,0:T(8,128)} %ids_hbm.1, bf16[64,512]{1,0:T(8,128)(2,1)} %weight_hbm.1, s32[1,64]{1,0:T(1,128)} %bitcast.13), custom_call_target="tpu_custom_call" | custom-call | tf_op jit(solution)/shard_map/pack/pallas_call | solution.py:425
  4.1 7.3 %all-to-all-start = ((s32[8,64,128]{2,1,0:T(8,128)}), s32[8,64,128]{2,1,0:T(8,128)S(1)}, u32[]{:S(2)}, u32[]{:S(2)}) async-start(s32[8,64,128]{2,1,0:T(8,128)} %pack.1), calls=%async_computation | async-start | bytes 524288 | tf_op jit(solution)/shard_map/all_to_all | solution.py:439
  11.4 6.3 %prepare.1 = (f32[64,19008]{1,0:T(8,128)}, f32[64,19008]{1,0:T(8,128)}, f32[64,128]{1,0:T(8,128)S(1)}, f32[64,128]{1,0:T(8,128)S(1)}) custom-call(f32[64,19008]{1,0:T(8,128)} %logits_hbm.1, f32[1,64]{1,0:T(1,128)} %bitcast.10, f32[1,64]{1,0:T(1,128)} %bitcast.11, f32[1,64]{1,0:T(1,128)} %bitcast.12), custom_call_target="tpu_custom_call" | custom-call | flops 486604800 | bytes 486604800 | tf_op jit(solution)/shard_map/prepare/pallas_call | solution.py:451
  17.8 2.6 %all-to-all-done.got_ref = s32[8,64,128]{2,1,0:T(8,128)S(1)} async-done(((s32[8,64,128]{2,1,0:T(8,128)}), s32[8,64,128]{2,1,0:T(8,128)S(1)}, u32[]{:S(2)}, u32[]{:S(2)}) %all-to-all-start) | async-done | bytes 262176 | tf_op jit(solution)/shard_map/all_to_all | solution.py:439
  20.4 6.5 %tally.1 = (f32[64,19008]{1,0:T(8,128)S(1)}, f32[8,128]{1,0:T(8,128)S(1)}) custom-call(s32[8,64,128]{2,1,0:T(8,128)S(1)} %all-to-all-done.got_ref, f32[64,19008]{1,0:T(8,128)} %get-tuple-element.11.plain_hbm, f32[64,19008]{1,0:T(8,128)} %get-tuple-element.12.seen_hbm, f32[64,128]{1,0:T(8,128)S(1)} %get-tuple-element.13.shift_ref, ...), custom_call_target="tpu_custom_call" | custom-call | tf_op jit(solution)/shard_map/tally/pallas_call | solution.py:482
  26.8 9.9 %all_to_all.16 = f32[8,1,128]{2,1,0:T(1,128)S(1)} all-to-all(f32[8,1,128]{2,1,0:T(1,128)S(1)} %bitcast.9), channel_id=1, replica_groups=mesh['batch'=4,'vocab'=8] {'vocab'}, dimensions={0} | all-to-all | bytes 8192 | tf_op jit(solution)/shard_map/all_to_all | solution.py:500
  36.7 2.7 %finish.1 = f32[64,19008]{1,0:T(8,128)} custom-call(f32[64,19008]{1,0:T(8,128)S(1)} %get-tuple-element.15.adjusted_ref, f32[64,128]{1,0:T(8,128)S(1)} %get-tuple-element.13.shift_ref, f32[8,128]{1,0:T(8,128)S(1)} %bitcast.8), custom_call_target="tpu_custom_call" | custom-call | tf_op jit(solution)/shard_map/finish/pallas_call | solution.py:501
Async XLA Ops:
  4.1 16.2 %all-to-all-start = ((s32[8,64,128]{2,1,0:T(8,128)}), s32[8,64,128]{2,1,0:T(8,128)S(1)}, u32[]{:S(2)}, u32[]{:S(2)}) async-start(s32[8,64,128]{2,1,0:T(8,128)} %pack.1), calls=%async_computation | async-start | bytes 524288 | tf_op jit(solution)/shard_map/all_to_all | solution.py:439

commit v2 on v1

--- a/solution.py
+++ b/solution.py
@@ -151,16 +151,16 @@
     for group in range(groups):
         loads[group].wait()
         part = slice(group * 8, group * 8 + 8)
-        best = jnp.full((8, LANES), -jnp.inf, jnp.float32)
+        bests = [jnp.full((8, LANES), -jnp.inf, jnp.float32)] * 8
         tail = None
         for tile in range(tiles):
             size = min(LANES, width - tile * LANES)
             x = logits[part, tile * LANES : tile * LANES + size]
             if size == LANES:
-                best = jnp.maximum(best, x)
+                bests[tile % 8] = jnp.maximum(bests[tile % 8], x)
             else:
                 tail = jnp.max(x, axis=1, keepdims=True)
-        top = jnp.max(best, axis=1, keepdims=True)
+        top = jnp.max(functools.reduce(jnp.maximum, bests), axis=1, keepdims=True)
         if tail is not None:
             top = jnp.maximum(top, tail)
         shift = top * LOG2E

time: 39.9 us -> 39.9 us (level)
  blocking collectives: 9.87 us -> 9.36 us
  Pallas kernels: 19.6 us -> 20 us
    pallas_call x1, Pallas kernels: 6.47 us -> 7.01 us  [body(): pl.pallas_call(functools.partial(tally_kernel, ordered), out_shape=(wide,...]
    all_to_all x1, blocking collectives: 9.87 us -> 9.36 us  [body(): lax.all_to_all(stats, 'vocab', split_axis=0, concat_axis=0, tiled=True)]
where the time goes in v2:
time: 39.9 us; the launch traced here: 39.4 us
  Pallas kernels  20 us (50%)
  blocking collectives  9.36 us (23%)
  starting transfers between devices  7.32 us (18%)
  waiting for transfers between devices  2.72 us (7%)
    all_to_all x1, blocking collectives, body(): lax.all_to_all(stats, 'vocab', split_axis=0, concat_axis=0, tiled=True)  9.36 us
    all_to_all x1, starting transfers between devices, body(): got = lax.all_to_all(send, 'vocab', split_axis=0, concat_axis=0, tiled=True)  7.32 us
    pallas_call x1, Pallas kernels, body(): pl.pallas_call(functools.partial(tally_kernel, ordered), out_shape=(wide,...  7.01 us
    pallas_call x1, Pallas kernels, body(): pl.pallas_call(prepare_kernel, out_shape=(pltpu.HBM((rows, width), jnp.fl...  6.19 us
    pallas_call x1, Pallas kernels, body(): pl.pallas_call(functools.partial(pack_kernel, shards, slots, width), out_...  4.11 us
    all_to_all x1, waiting for transfers between devices, body(): got = lax.all_to_all(send, 'vocab', split_axis=0, concat_axis=0, tiled=True)  2.72 us
    pallas_call x1, Pallas kernels, body(): pl.pallas_call(finish_kernel, out_shape=jax.ShapeDtypeStruct((rows, width...  2.68 us
  transfers between devices with their start and end apart: 1, of which 1 were waited for; matrix products, arithmetic and copies ran while one was open for 0% of the time, Pallas kernels for 16%

profile of v2, /device:TPU:0, one launch (start us, length us, event | category | flops | bytes accessed | tf_op | source)
XLA Modules:
  0.0 39.4 jit_solution(1420844229599652419)
XLA Ops:
  0.0 4.1 %pack.1 = s32[8,64,128]{2,1,0:T(8,128)} custom-call(s32[64,512]{1,0:T(8,128)} %ids_hbm.1, bf16[64,512]{1,0:T(8,128)(2,1)} %weight_hbm.1, s32[1,64]{1,0:T(1,128)} %bitcast.13), custom_call_target="tpu_custom_call" | custom-call | tf_op jit(solution)/shard_map/pack/pallas_call | solution.py:425
  4.1 7.3 %all-to-all-start = ((s32[8,64,128]{2,1,0:T(8,128)}), s32[8,64,128]{2,1,0:T(8,128)S(1)}, u32[]{:S(2)}, u32[]{:S(2)}) async-start(s32[8,64,128]{2,1,0:T(8,128)} %pack.1), calls=%async_computation | async-start | bytes 524288 | tf_op jit(solution)/shard_map/all_to_all | solution.py:439
  11.4 6.2 %prepare.1 = (f32[64,19008]{1,0:T(8,128)}, f32[64,19008]{1,0:T(8,128)}, f32[64,128]{1,0:T(8,128)S(1)}, f32[64,128]{1,0:T(8,128)S(1)}) custom-call(f32[64,19008]{1,0:T(8,128)} %logits_hbm.1, f32[1,64]{1,0:T(1,128)} %bitcast.10, f32[1,64]{1,0:T(1,128)} %bitcast.11, f32[1,64]{1,0:T(1,128)} %bitcast.12), custom_call_target="tpu_custom_call" | custom-call | flops 486604800 | bytes 486604800 | tf_op jit(solution)/shard_map/prepare/pallas_call | solution.py:451
  17.6 2.7 %all-to-all-done.got_ref = s32[8,64,128]{2,1,0:T(8,128)S(1)} async-done(((s32[8,64,128]{2,1,0:T(8,128)}), s32[8,64,128]{2,1,0:T(8,128)S(1)}, u32[]{:S(2)}, u32[]{:S(2)}) %all-to-all-start) | async-done | bytes 262176 | tf_op jit(solution)/shard_map/all_to_all | solution.py:439
  20.4 7.0 %tally.1 = (f32[64,19008]{1,0:T(8,128)S(1)}, f32[8,128]{1,0:T(8,128)S(1)}) custom-call(s32[8,64,128]{2,1,0:T(8,128)S(1)} %all-to-all-done.got_ref, f32[64,19008]{1,0:T(8,128)} %get-tuple-element.11.plain_hbm, f32[64,19008]{1,0:T(8,128)} %get-tuple-element.12.seen_hbm, f32[64,128]{1,0:T(8,128)S(1)} %get-tuple-element.13.shift_ref, ...), custom_call_target="tpu_custom_call" | custom-call | tf_op jit(solution)/shard_map/tally/pallas_call | solution.py:482
  27.4 9.4 %all_to_all.16 = f32[8,1,128]{2,1,0:T(1,128)S(1)} all-to-all(f32[8,1,128]{2,1,0:T(1,128)S(1)} %bitcast.9), channel_id=1, replica_groups=mesh['batch'=4,'vocab'=8] {'vocab'}, dimensions={0} | all-to-all | bytes 8192 | tf_op jit(solution)/shard_map/all_to_all | solution.py:500
  36.7 2.7 %finish.1 = f32[64,19008]{1,0:T(8,128)} custom-call(f32[64,19008]{1,0:T(8,128)S(1)} %get-tuple-element.15.adjusted_ref, f32[64,128]{1,0:T(8,128)S(1)} %get-tuple-element.13.shift_ref, f32[8,128]{1,0:T(8,128)S(1)} %bitcast.8), custom_call_target="tpu_custom_call" | custom-call | tf_op jit(solution)/shard_map/finish/pallas_call | solution.py:501
Async XLA Ops:
  4.1 16.2 %all-to-all-start = ((s32[8,64,128]{2,1,0:T(8,128)}), s32[8,64,128]{2,1,0:T(8,128)S(1)}, u32[]{:S(2)}, u32[]{:S(2)}) async-start(s32[8,64,128]{2,1,0:T(8,128)} %pack.1), calls=%async_computation | async-start | bytes 524288 | tf_op jit(solution)/shard_map/all_to_all | solution.py:439
